TPU v7x, 32 devices: a whole 2x2x4 slice. The times are simulated.
32 devices in a mesh: row: 16 (over z, y, core), col: 2 (over x).
Axes of the slice: x: 2, y: 2, z: 4, core: 2. Of those that a mesh axis runs over, the one named last changes fastest.
Arguments:
- row_embed: bfloat16 [300, 16384], P(None, 'row'), may hold values from -1.796875 to 1.796875
- col_embed: bfloat16 [300, 2, 256], P(None, 'col', 'row'), may hold values from -1.796875 to 1.796875
- counts: int32 [16384, 2, 256], P('row', 'col'), may hold values from 0 to 64, as said below
- occupancy: int32 [128, 2, 2], P('row', 'col'), may hold values from 0 to 1, as said below
- row_marg: int32 [16384], P('row'), may hold values from 2000 to 199999
- col_marg: int32 [2, 256], P('col', 'row'), may hold values from 2000 to 199999
- log_total: float32 [1], replicated, may hold values from 18 to 22
Outputs:
- grad_rows: float32 [300, 16384], P(None, 'row')
- grad_cols: float32 [300, 2, 256], P(None, 'col', 'row')
Inputs may be any that keep to these rules, and one draw needn't show every extreme that they name: counts of the band's cells; zero in part of the cells. `occupancy`: the share of tiles marked 1 differs from row tile to row tile.
All inputs are finite; a program needn't handle non-finite values.
Results may differ from a plain program's by a relative error of at most 0.0018.
Values may be sent and summed in bfloat16 or wider, within the bound.
A program may use at most 64 MiB of HBM per device.

v0:
```python
import math

import jax
import jax.numpy as jnp
from jax import lax
from jax.sharding import PartitionSpec as P


def cell_slope(scores, count_piece, log_row, log_piece, log_base):
    count_values = count_piece.astype(jnp.float32)
    log_ratio = jnp.log(jnp.maximum(count_values, 1.0)) + (
        log_base - log_row[:, None] - log_piece[None, :]
    )
    score_gap = scores - log_ratio
    return jnp.where(
        count_piece > 0,
        (0.1 + 0.25 * jnp.sqrt(count_values)) * score_gap,
        jax.nn.sigmoid(score_gap),
    )


def band_residual(row_embed, cols_piece, count_piece, occ_float, log_row, log_piece, log_base):
    piece_width = cols_piece.shape[1]
    row_tiles = occ_float.shape[0]
    band_tiles = occ_float.shape[1]
    tile_size = row_embed.shape[1] // row_tiles
    scores = jnp.einsum("di,dj->ij", row_embed, cols_piece, preferred_element_type=jnp.float32)
    slopes = cell_slope(scores, count_piece, log_row, log_piece, log_base)
    tile_index = jnp.arange(piece_width, dtype=jnp.int32) // tile_size
    selector = (tile_index[None, :] == jnp.arange(band_tiles, dtype=jnp.int32)[:, None]).astype(
        jnp.float32
    )
    col_mask = jnp.dot(occ_float, selector, preferred_element_type=jnp.float32)
    masked = slopes.reshape(row_tiles, tile_size, piece_width) * col_mask[:, None, :]
    return masked.reshape(-1, piece_width).astype(jnp.bfloat16)


def body(row_embed, col_embed, counts, occupancy, row_marg, col_marg, log_total):
    rows_dev = row_embed.shape[1]
    cols_local = col_embed.shape[2]
    total_rows = rows_dev * lax.axis_size("row")
    total_cols = cols_local * lax.axis_size("row") * lax.axis_size("col")
    local_counts = counts[:, 0, :]
    occ_float = occupancy[:, 0, :].astype(jnp.float32)
    log_row = jnp.log(row_marg.astype(jnp.float32))
    log_base = log_total[0]
    marg_shard = col_marg[None]
    gathered, marg_all = (
        lax.all_gather(col_embed, "row", axis=2, tiled=True),
        lax.all_gather(marg_shard, "row", axis=2, tiled=True),
    )
    band_cols = gathered[:, 0, :]
    log_col = jnp.log(marg_all[0, 0].astype(jnp.float32))
    residual = band_residual(
        row_embed, band_cols, local_counts, occ_float, log_row, log_col, log_base
    )
    partial_rows = jnp.einsum("dj,ij->di", band_cols, residual, preferred_element_type=jnp.float32)
    owned = lax.psum_scatter(
        jnp.einsum("ij,di->jd", residual, row_embed, preferred_element_type=jnp.float32),
        "row",
        scatter_dimension=0,
        tiled=True,
    )
    summed_cols = owned.T[:, None, :]
    summed_rows = lax.psum(partial_rows, "col")
    grad_rows = summed_rows * (1.0 / math.sqrt(total_cols))
    grad_cols = summed_cols * (1.0 / math.sqrt(total_rows))
    return (grad_rows, grad_cols)


def solution(mesh):
    placed = (
        P(None, "row"),
        P(None, "col", "row"),
        P("row", "col", None),
        P("row", "col", None),
        P("row"),
        P("col", "row"),
        P(),
    )
    return jax.shard_map(
        body,
        mesh=mesh,
        in_specs=placed,
        out_specs=(P(None, "row"), P(None, "col", "row")),
        check_vma=False,
    )
```

profile of v0, /device:TPU:0, one launch (start us, length us, event | category | flops | bytes accessed | tf_op | source)
XLA Modules:
  0.0 114.4 jit_solution(9142575697323880410)
XLA Ops:
  8.0 0.0 copy-start
  8.0 0.0 reduce-scatter.2.cloned.1.call-start
  8.8 1.2 %dynamic-slice = u32[1]{0:T(128)} dynamic-slice(u32[32]{0:T(128)} %constant.35, u32[]{:T(128)S(6)} %add.29), dynamic_slice_sizes={1} | dynamic-slice | bytes 12
  10.7 0.8 bitcast_dynamic-update-slice_fusion
  11.4 13.8 %all-reduce = s32[256]{0:T(256)S(1)} all-reduce(s32[256]{0:T(256)S(1)} %bitcast_dynamic-update-slice_fusion), channel_id=2, replica_groups=mesh['row'=16,'col'=2] {'row'}, use_global_device_ids=true, to_apply=%add | all-reduce | flops 256 | bytes 2048
  25.2 18.7 %all_gather.6 = bf16[300,1,256]{0,2,1:T(8,128)(2,1)S(1)} all-gather(bf16[300,1,16]{0,2,1:T(8,128)(2,1)} %param.8), channel_id=1, replica_groups=mesh['row'=16,'col'=2] {'row'}, dimensions={2}, use_global_device_ids=true | all-gather | bytes 163200 | tf_op jit(solution)/shard_map/all_gather | solution.py:49
  43.9 0.7 log_subtract_fusion
  44.6 0.9 convolution_bitcast_fusion.1
  45.5 0.0 copy-done
  45.5 2.3 %fusion = bf16[1024,256]{1,0:T(8,128)(2,1)S(1)} fusion(bf16[300,1024]{1,0:T(8,128)(2,1)S(1)} %copy-done, s32[1024,1,256]{2,1,0:T(1,128)} %param.9, f32[256]{0:T(256)S(1)} %convert_log_fusion, f32[8,256]{1,0:T(8,128)S(1)} %convolution_bitcast_fusion.1, f32[1024]{0:T(1024)S(1)} %log_subtract_fusion, bf16[300,1,256]{0,2,1:T(8,128)(2,1)S(1)} %all_gather.6), kind=kOutput, calls=%fused_computation.4 | convolution fusion | flops 161218560 | bytes 2354176 | tf_op jit(solution)/shard_map/di,dj->ij/dot_general | solution.py:27
  47.8 1.3 %fusion.9 = f32[256,300]{1,0:T(8,128)} fusion(bf16[1024,256]{1,0:T(8,128)(2,1)S(1)} %fusion, bf16[300,1024]{1,0:T(8,128)(2,1)S(1)} %copy-done), kind=kOutput, calls=%fused_computation.24 | convolution fusion | flops 157286400 | bytes 1445888 | tf_op jit(solution)/shard_map/ij,di->jd/dot_general | solution.py:59
  49.1 0.0 reduce-scatter.2.cloned.1.call-update
  49.1 0.0 all-reduce.3.cloned.1.call-start
  49.2 1.4 %convolution_bitcast_fusion = f32[300,1024]{1,0:T(8,128)} fusion(bf16[1024,256]{1,0:T(8,128)(2,1)S(1)} %fusion, bf16[300,1,256]{0,2,1:T(8,128)(2,1)S(1)} %all_gather.6), kind=kOutput, calls=%fused_computation | convolution fusion | flops 157286400 | bytes 1906688 | tf_op jit(solution)/shard_map/dj,ij->di/dot_general | solution.py:57
  50.6 0.0 all-reduce.3.cloned.1.call-update
  50.6 52.5 %reduce-scatter.2.cloned.1.call-done = f32[16,300]{1,0:T(8,128)} async-done(((f32[256,300]{1,0:T(8,128)}), f32[16,300]{1,0:T(8,128)}) %reduce-scatter.2.cloned.1.call-update) | async-done | bytes 19216 | tf_op jit(solution)/shard_map/reduce_scatter | solution.py:58
  103.1 1.3 %multiply_bitcast_fusion = f32[300,1,16]{0,2,1:T(8,128)} fusion(f32[16,300]{1,0:T(8,128)} %reduce-scatter.2.cloned.1.call-done), kind=kLoop, calls=%fused_computation.11 | loop fusion | flops 4800 | bytes 38400 | tf_op jit(solution)/shard_map/mul | solution.py:67
  104.4 0.0 all-reduce.3.cloned.1.call-done
  104.4 2.5 %broadcast_multiply_fusion = f32[300,1024]{1,0:T(8,128)} fusion(f32[300,1024]{1,0:T(8,128)} %all-reduce.3.cloned.1.call-done), kind=kLoop, calls=%fused_computation.8 | loop fusion | flops 307200 | bytes 2457600 | tf_op jit(solution)/shard_map/mul | solution.py:66
  (3 shorter events, 0.0 us)
Async XLA Ops:
  8.0 37.5 %copy-start = (bf16[300,1024]{1,0:T(8,128)(2,1)S(1)}, bf16[300,1024]{1,0:T(8,128)(2,1)}, u32[]{:S(2)}) copy-start(bf16[300,1024]{1,0:T(8,128)(2,1)} %param.7) | copy-start | bytes 1843204
  8.0 95.1 %reduce-scatter.2.cloned.1.call-start = ((), (), s32[]{:S(2)}) async-start(), calls=%async_computation.2 | async-start | bytes 417792 | tf_op jit(solution)/shard_map/reduce_scatter | solution.py:58
  49.1 55.3 %all-reduce.3.cloned.1.call-start = ((), (), s32[]{:S(2)}) async-start(), calls=%async_computation.1 | async-start | bytes 2490368 | tf_op jit(solution)/shard_map/psum | solution.py:65
Sparse Core Ops, SparseCore 0:
  49.2 53.8 reduce-scatter.1
Sparse Core Ops, SparseCore 1:
  52.5 42.0 all-reduce.2
where the time goes:
time: 115 us; the launch traced here: 114 us
  waiting for transfers between devices  52.5 us (46%)
  blocking collectives  32.5 us (28%)
  between operations  16.9 us (15%)
  matrix products  5.86 us (5%)
  other arithmetic  4.57 us (4%)
  local copies, waits for them, and re-layouts  2.01 us (2%)
    reduce_scatter x1, waiting for transfers between devices, body(): lax.psum_scatter(jnp.einsum('ij,di->jd', residual, row_embed, preferred_e...  52.5 us
    all_gather x1, blocking collectives, body(): lax.all_gather(col_embed, 'row', axis=2, tiled=True)  18.7 us
    unnamed x1, blocking collectives  13.8 us
    mul x1, other arithmetic, body(): grad_rows = summed_rows * (1.0 / math.sqrt(total_cols))  2.52 us
    dot_general x1, matrix products, band_residual(): jnp.einsum('di,dj->ij', row_embed, cols_piece, preferred_element_type=jnp...  2.33 us
  transfers between devices with their start and end apart: 2, of which 1 were waited for; matrix products, arithmetic and copies ran while one was open for 2% of the time, Pallas kernels for 0%

commit v1 on v0

v1 whole, which is shorter than its diff:
```python
import functools
import math

import jax
import jax.numpy as jnp
from jax import lax
from jax.experimental import pallas as pl
from jax.experimental.pallas import tpu as pltpu
from jax.sharding import PartitionSpec as P

LANES = 128
SEND = jnp.bfloat16


def nt(a, b):
    return lax.dot_general(a, b, (((1,), (1,)), ((), ())), preferred_element_type=jnp.float32)


def nn(a, b):
    return lax.dot_general(a, b, (((1,), (0,)), ((), ())), preferred_element_type=jnp.float32)


def split3(x):
    hi = x.astype(jnp.bfloat16).astype(jnp.float32)
    rest = x - hi
    mid = rest.astype(jnp.bfloat16).astype(jnp.float32)
    return hi, mid, rest - mid


def eye(n):
    r = lax.broadcasted_iota(jnp.int32, (n, n), 0)
    c = lax.broadcasted_iota(jnp.int32, (n, n), 1)
    return (r == c).astype(jnp.float32).astype(jnp.bfloat16)


def slope_terms(code):
    slope = jnp.where(code > 0.0, 0.1 + 0.25 * jnp.sqrt(jnp.maximum(code, 0.0)), 0.0)
    return slope, jnp.log(jnp.maximum(code, 1.0))


def cell(code, slope, logc, gap):
    return jnp.where(code == 0.0, jax.nn.sigmoid(gap), slope * (gap - logc))


def repeat(n, fn):
    if n == 1:
        fn(0)
    else:
        pl.loop(0, n)(fn)


def kernel(cfg, r_hbm, c_ref, cnt_hbm, occ_ref, rm_ref, cm_ref, lt_ref,
           rows_out, cols_out,
           r_v, cnt_v, raug, blk, cg, cd, enc, slope_v, logc_v, res, gcol, s1buf, s2src, s2buf,
           dsem, gz_s, gz_r, gc_s, gc_r, gx_s, gx_r, e_s, e_r, a_s, a_r, b_s, b_r):
    n, d, dp, w, band, rows, tile, q_w, scale_r, scale_c = cfg
    half = n // 2
    nq = rows // q_w
    btiles = band // LANES
    sub = min(band, 256)
    nsub = band // sub
    me = lax.axis_index("row")
    col = lax.axis_index("col")
    core = lax.rem(me, 2)
    mate = me + 1 - 2 * core
    mine = me // 2
    peers = [lax.rem(me + 2 * k, n) for k in range(1, half)]
    froms = [lax.rem(me - 2 * k + n, n) for k in range(1, half)]
    at_mate = (mate, col)
    at_x = (me, 1 - col)

    def rcopy(src, dst, ss, rs, dev):
        return pltpu.make_async_remote_copy(
            src_ref=src, dst_ref=dst, send_sem=ss, recv_sem=rs,
            device_id=dev, device_id_type=pl.DeviceIdType.MESH)

    barrier = pltpu.get_barrier_semaphore()
    for dev in [(p, col) for p in peers] + [at_mate, at_x]:
        pl.semaphore_signal(barrier, inc=1, device_id=dev, device_id_type=pl.DeviceIdType.MESH)
    step = q_w * btiles
    loads = []
    for q in range(nq):
        cp = pltpu.make_async_copy(
            cnt_hbm.at[pl.ds(q * step, step), :], cnt_v.at[pl.ds(q * step, step), :], dsem.at[q])
        cp.start()
        loads.append(cp)
    rload = pltpu.make_async_copy(r_hbm, r_v, dsem.at[nq])
    rload.start()

    log_c = jnp.log(cm_ref[...].astype(jnp.float32))
    ri = lax.broadcasted_iota(jnp.int32, (w, w), 0)
    ci = lax.broadcasted_iota(jnp.int32, (w, w), 1)
    log_c = jnp.sum(jnp.where(ri == ci, jnp.broadcast_to(log_c, (w, w)), 0.0), axis=1, keepdims=True)
    hi, mid, lo = split3(log_c)
    blk[...] = jnp.zeros_like(blk)
    blk[:, pl.ds(0, d)] = c_ref[...].astype(jnp.float32)
    li = lax.broadcasted_iota(jnp.int32, (w, dp), 1)
    own = blk[...]
    for at, val in ((d, hi), (d + 1, mid), (d + 2, lo)):
        own = jnp.where(li == at, val, own)
    own = jnp.where((li >= d + 3) & (li < d + 6), 1.0, own)
    cg[0, me] = own.astype(jnp.bfloat16)

    ident = eye(LANES)

    def encode(q):
        loads[q].wait()

        def part(t):
            cells = []
            for u in range(q_w // tile):
                x = cnt_v[pl.ds(q * step + u * tile * btiles + t, tile, stride=btiles), :]
                on = occ_ref[t, q * (q_w // tile) + u] != 0
                cells.append(jnp.where(on, x, -1).astype(jnp.float32).astype(jnp.bfloat16))
            code = nt(ident, jnp.concatenate(cells, axis=0))
            at = pl.ds(t * LANES, LANES)
            enc[0, q, at, :] = code.astype(jnp.bfloat16)
            slope_v[q, at, :], logc_v[q, at, :] = slope_terms(code)

        for t in range(btiles):
            part(t)

    encode(0)
    pl.semaphore_wait(barrier, half + 1)

    xcp = rcopy(cg.at[0, me], cg.at[1, me], gx_s, gx_r, at_x)
    xcp.start()
    sends = [xcp]
    for p in peers:
        cp = rcopy(cg.at[0, me], cg.at[0, me], gz_s.at[0, p // 2], gz_r.at[0, mine], (p, col))
        cp.start()
        sends.append(cp)
    cp = rcopy(cg.at[0, me], cg.at[0, me], gc_s.at[0, mine], gc_r.at[0, mine], at_mate)
    cp.start()
    sends.append(cp)

    ecopies = [rcopy(enc.at[0, q], enc.at[1, q], e_s.at[q], e_r.at[q], at_x) for q in range(nq)]
    for q in range(1, nq):
        ecopies[q - 1].start()
        encode(q)

    rload.wait()
    raug[pl.ds(0, d), :] = r_v[...]
    first = (d // 16) * 16
    row_term = jnp.log(rm_ref[...].astype(jnp.float32)) - lt_ref[0]
    hi, mid, lo = split3(row_term)
    tail = raug[pl.ds(first, dp - first), :].astype(jnp.float32)
    si = lax.broadcasted_iota(jnp.int32, (dp - first, rows), 0) + first
    tail = jnp.where(si < d, tail, jnp.where(si < d + 3, 1.0, 0.0))
    for at, val in ((d + 3, hi), (d + 4, mid), (d + 5, lo)):
        tail = jnp.where(si == at, val, tail)
    raug[pl.ds(first, dp - first), :] = tail.astype(jnp.bfloat16)
    ecopies[nq - 1].start()

    xcp.wait_recv()
    for p in peers:
        cp = rcopy(cg.at[1, me], cg.at[1, me], gz_s.at[1, p // 2], gz_r.at[1, mine], (p, col))
        cp.start()
        sends.append(cp)
    cp = rcopy(cg.at[1, me], cg.at[1, me], gc_s.at[1, mine], gc_r.at[1, mine], at_mate)
    cp.start()
    sends.append(cp)

    def forward(which):
        for p in froms:
            rcopy(cg.at[which, p], cg.at[which, p], gz_s.at[which, p // 2],
                  gz_r.at[which, p // 2], at_mate).wait_recv()
            cp = rcopy(cg.at[which, p], cg.at[which, p], gc_s.at[which, p // 2],
                       gc_r.at[which, p // 2], at_mate)
            cp.start()
            sends.append(cp)

    def mate_blocks(which):
        for k in range(half):
            at = 2 * k + 1 - core
            rcopy(cg.at[which, at], cg.at[which, at], gc_s.at[which, k],
                  gc_r.at[which, k], at_mate).wait_recv()

    forward(0)
    mate_blocks(0)

    per = sub // w

    def block(which, s):
        return cg[which, pl.ds(s * per, per)].reshape(sub, dp)

    for q in range(nq):
        qs = pl.ds(q * q_w, q_w)

        def cells(s):
            at = pl.ds(s * sub, sub)
            gap = nn(block(0, s), raug[:, qs])
            code = enc[0, q, at, :].astype(jnp.float32)
            res[at, qs] = cell(code, slope_v[q, at, :], logc_v[q, at, :], gap).astype(jnp.bfloat16)

        repeat(nsub, cells)

    def col_terms(s):
        gcol[pl.ds(s * per, per)] = nt(res[pl.ds(s * sub, sub), :], raug[...]).reshape(per, w, dp)

    repeat(nsub, col_terms)
    for k in range(half):
        cp = rcopy(gcol.at[2 * k + 1 - core], s1buf.at[k], a_s.at[k], a_r.at[k], at_mate)
        cp.start()
        sends.append(cp)

    ident_d = eye(dp)

    def transposed(which):
        def one(s):
            cd[which, :, pl.ds(s * sub, sub)] = nt(ident_d, block(which, s)).astype(jnp.bfloat16)

        repeat(nsub, one)

    transposed(0)
    rows_out[...] = nn(cd[0], res[...])[:d, :]

    forward(1)
    for k in range(half):
        rcopy(gcol.at[k], s1buf.at[k], a_s.at[k], a_r.at[k], at_mate).wait_recv()
    for p in peers:
        s2src[p // 2] = (gcol[p] + s1buf[p // 2]).astype(s2src.dtype)
    total = gcol[me] + s1buf[mine]
    mate_blocks(1)
    for p in peers:
        cp = rcopy(s2src.at[p // 2], s2buf.at[mine], b_s.at[p // 2], b_r.at[mine], (p, col))
        cp.start()
        sends.append(cp)

    transposed(1)
    for q in range(nq):
        qs = pl.ds(q * q_w, q_w)
        ecopies[q].wait_recv()

        def cells(s):
            at = pl.ds(s * sub, sub)
            gap = nn(block(1, s), raug[:, qs])
            code = enc[1, q, at, :].astype(jnp.float32)
            slope, logc = slope_terms(code)
            res[at, qs] = cell(code, slope, logc, gap).astype(jnp.bfloat16)

        repeat(nsub, cells)
        rows_out[:, qs] = (rows_out[:, qs] + nn(cd[1], res[:, qs])[:d, :]) * scale_r

    for p in froms:
        rcopy(s2src.at[0], s2buf.at[p // 2], b_s.at[p // 2], b_r.at[p // 2], at_mate).wait_recv()
        total = total + s2buf[p // 2].astype(jnp.float32)
    cols_out[...] = (total * scale_c)[:, :d]
    for cp in sends + ecopies:
        cp.wait_send()


def body(row_embed, col_embed, counts, occupancy, row_marg, col_marg, log_total):
    n = lax.axis_size("row")
    d, rows = row_embed.shape
    w = col_embed.shape[2]
    band = counts.shape[2]
    tile = rows // occupancy.shape[0]
    q_w = 2 * tile if rows % (2 * tile) == 0 else tile
    dp = -(-(d + 6) // LANES) * LANES
    half = n // 2
    nq = rows // q_w
    btiles = band // LANES
    cfg = (n, d, dp, w, band, rows, tile, q_w,
           1.0 / math.sqrt(w * n * lax.axis_size("col")), 1.0 / math.sqrt(rows * n))
    bf, f32 = jnp.bfloat16, jnp.float32
    vm, sm, hb = (pl.BlockSpec(memory_space=m) for m in (pltpu.VMEM, pltpu.SMEM, pl.ANY))
    dma = lambda *s: pltpu.SemaphoreType.DMA(s) if s else pltpu.SemaphoreType.DMA
    grad_rows, grad_cols = pl.pallas_call(
        functools.partial(kernel, cfg),
        out_shape=(jax.ShapeDtypeStruct((d, rows), f32), jax.ShapeDtypeStruct((w, d), f32)),
        in_specs=[hb, vm, hb, sm, vm, vm, sm],
        out_specs=(vm, vm),
        scratch_shapes=[
            pltpu.VMEM((d, rows), bf),
            pltpu.VMEM((rows * btiles, LANES), jnp.int32),
            pltpu.VMEM((dp, rows), bf),
            pltpu.VMEM((w, dp), f32),
            pltpu.VMEM((2, n, w, dp), bf),
            pltpu.VMEM((2, dp, band), bf),
            pltpu.VMEM((2, nq, band, q_w), bf),
            pltpu.VMEM((nq, band, q_w), f32),
            pltpu.VMEM((nq, band, q_w), f32),
            pltpu.VMEM((band, rows), bf),
            pltpu.VMEM((n, w, dp), f32),
            pltpu.VMEM((half, w, dp), f32),
            pltpu.VMEM((half, w, dp), SEND),
            pltpu.VMEM((half, w, dp), SEND),
            dma(nq + 1),
            dma(2, half), dma(2, half), dma(2, half), dma(2, half), dma(), dma(),
            dma(nq), dma(nq), dma(half), dma(half), dma(half), dma(half),
        ],
        compiler_params=pltpu.CompilerParams(
            collective_id=0, has_side_effects=True, vmem_limit_bytes=60 * 1024 * 1024),
    )(
        row_embed,
        jnp.transpose(col_embed, (1, 2, 0)).reshape(w, d),
        counts.reshape(rows * btiles, LANES),
        jnp.transpose(occupancy, (1, 2, 0)).reshape(occupancy.shape[2], occupancy.shape[0]),
        row_marg.reshape(1, rows),
        col_marg,
        log_total,
    )
    return grad_rows, jnp.transpose(grad_cols.reshape(1, w, d), (2, 0, 1))


def solution(mesh):
    placed = (
        P(None, "row"),
        P(None, "col", "row"),
        P("row", "col", None),
        P("row", "col", None),
        P("row"),
        P("col", "row"),
        P(),
    )
    return jax.shard_map(
        body,
        mesh=mesh,
        in_specs=placed,
        out_specs=(P(None, "row"), P(None, "col", "row")),
        check_vma=False,
    )
```

time: 115 us -> 27.6 us (0.24)
  waiting for transfers between devices: 52.5 us -> 0 us
  blocking collectives: 32.5 us -> 0 us
  Pallas kernels: 0 us -> 23 us
  between operations: 16.9 us -> 1.3 us
  matrix products: 5.86 us -> 0 us
  other arithmetic: 4.57 us -> 0 us
    reduce_scatter x1 -> x0, waiting for transfers between devices: 52.5 us -> none  [body(): lax.psum_scatter(jnp.einsum('ij,di->jd', residual, row_embed, preferred_e...]
    pallas_call x0 -> x1, Pallas kernels: none -> 23 us  [body(): pl.pallas_call(functools.partial(kernel, cfg), out_shape=(jax.ShapeDtypeS...]
    all_gather x1 -> x0, blocking collectives: 18.7 us -> none  [body(): lax.all_gather(col_embed, 'row', axis=2, tiled=True)]
    unnamed x1 -> x0, blocking collectives: 13.8 us -> none
    dot_general x4 -> x0, matrix products: 5.86 us -> none  [the longest x1 2.33 us: band_residual(): jnp.einsum('di,dj->ij', row_embed, cols_piece, preferred_element_type=jnp...]
    mul x2 -> x0, other arithmetic: 3.86 us -> none  [the longest x1 2.52 us: body(): grad_rows = summed_rows * (1.0 / math.sqrt(total_cols))]
    unnamed x5 -> x4, local copies, waits for them, and re-layouts: 2.01 us -> 3.08 us
  transfers between devices with their start and end apart: 2 -> 0, of which waited for: 1 -> 0; matrix products, arithmetic and copies ran while one was open for 2% -> 0% of each run, Pallas kernels for 0% -> 0%
where the time goes in v1:
time: 27.6 us; the launch traced here: 27.4 us
  Pallas kernels  23 us (83%)
  local copies, waits for them, and re-layouts  3.08 us (11%)
  between operations  1.3 us (5%)
    pallas_call x1, Pallas kernels, body(): pl.pallas_call(functools.partial(kernel, cfg), out_shape=(jax.ShapeDtypeS...  23 us
    unnamed x4, local copies, waits for them, and re-layouts  3.08 us

profile of v1, /device:TPU:0, one launch (start us, length us, event | category | flops | bytes accessed | tf_op | source)
XLA Modules:
  0.0 27.4 jit_solution(15776487599343447372)
XLA Ops:
  1.3 23.0 %shard_map.86 = (f32[300,1024]{1,0:T(8,128)}, f32[16,300]{1,0:T(8,128)}) custom-call(bf16[300,1024]{1,0:T(8,128)(2,1)} %r_hbm.1, bf16[16,300]{1,0:T(8,128)(2,1)} %bitcast.13, s32[2048,128]{1,0:T(8,128)} %bitcast.11, s32[2,8]{1,0:T(2,128)} %bitcast.15, s32[1,1024]{1,0:T(1,128)} %bitcast.14, s32[1,16]{1,0:T(1,128)} %cm_ref.1, f32[1]{0:T(128)S(6)} %copy.11.lt_ref), custom_call_target="tpu_custom_call" | custom-call | tf_op jit(solution)/shard_map/pallas_call | solution.py:269
  24.3 0.0 copy-start
  24.3 2.5 %copy.12 = f32[300,1024]{1,0:T(8,128)} copy(f32[300,1024]{1,0:T(8,128)} %get-tuple-element.8) | data formatting | bytes 2457600
  26.8 0.0 copy-done
  26.8 0.6 %copy.13 = f32[300,1,16]{0,2,1:T(8,128)} copy(f32[300,1,16]{0,2,1:T(8,128)S(1)} %bitcast.12) | data formatting | bytes 38400
Async XLA Ops:
  24.3 2.5 %copy-start = (f32[16,300]{1,0:T(8,128)S(1)}, f32[16,300]{1,0:T(8,128)}, u32[]{:S(2)}) copy-start(f32[16,300]{1,0:T(8,128)} %get-tuple-element.5) | copy-start | bytes 57604

commit v2 on v1

--- a/solution.py
+++ b/solution.py
@@ -49,10 +49,10 @@
         pl.loop(0, n)(fn)
 
 
-def kernel(cfg, r_hbm, c_ref, cnt_hbm, occ_ref, rm_ref, cm_ref, lt_ref,
+def kernel(cfg, r_hbm, c_hbm, cnt_hbm, occ_hbm, rm_hbm, cm_hbm, lt_ref,
            rows_out, cols_out,
            r_v, cnt_v, raug, blk, cg, cd, enc, slope_v, logc_v, res, gcol, s1buf, s2src, s2buf,
-           dsem, gz_s, gz_r, gc_s, gc_r, gx_s, gx_r, e_s, e_r, a_s, a_r, b_s, b_r):
+           c_ref, occ_ref, rm_ref, cm_ref, dsem, gz_s, gz_r, gc_s, gc_r, gx_s, gx_r, e_s, e_r, a_s, a_r, b_s, b_r):
     n, d, dp, w, band, rows, tile, q_w, scale_r, scale_c = cfg
     half = n // 2
     nq = rows // q_w
@@ -77,6 +77,12 @@
     barrier = pltpu.get_barrier_semaphore()
     for dev in [(p, col) for p in peers] + [at_mate, at_x]:
         pl.semaphore_signal(barrier, inc=1, device_id=dev, device_id_type=pl.DeviceIdType.MESH)
+    small = []
+    for k, (src, dst) in enumerate(((cm_hbm, cm_ref), (c_hbm, c_ref), (occ_hbm, occ_ref),
+                                    (rm_hbm, rm_ref))):
+        cp = pltpu.make_async_copy(src, dst, dsem.at[nq + 1 + k])
+        cp.start()
+        small.append(cp)
     step = q_w * btiles
     loads = []
     for q in range(nq):
@@ -86,6 +92,9 @@
         loads.append(cp)
     rload = pltpu.make_async_copy(r_hbm, r_v, dsem.at[nq])
     rload.start()
+
+    for cp in small:
+        cp.wait()
 
     log_c = jnp.log(cm_ref[...].astype(jnp.float32))
     ri = lax.broadcasted_iota(jnp.int32, (w, w), 0)
@@ -110,7 +119,8 @@
             cells = []
             for u in range(q_w // tile):
                 x = cnt_v[pl.ds(q * step + u * tile * btiles + t, tile, stride=btiles), :]
-                on = occ_ref[t, q * (q_w // tile) + u] != 0
+                k = q * (q_w // tile) + u
+                on = jnp.broadcast_to(occ_ref[t:t + 1, k:k + 1], (tile, LANES)) != 0
                 cells.append(jnp.where(on, x, -1).astype(jnp.float32).astype(jnp.bfloat16))
             code = nt(ident, jnp.concatenate(cells, axis=0))
             at = pl.ds(t * LANES, LANES)
@@ -248,6 +258,19 @@
     cols_out[...] = (total * scale_c)[:, :d]
     for cp in sends + ecopies:
         cp.wait_send()
+
+
+def scratch_bytes(shapes):
+    return sum(math.prod(s.shape) * jnp.dtype(s.dtype).itemsize for s in shapes)
+
+
+def place(rows_in, cols_in, rows_out, cols_out, sem):
+    copies = [pltpu.make_async_copy(rows_in, rows_out, sem.at[0]),
+              pltpu.make_async_copy(cols_in, cols_out, sem.at[1])]
+    for cp in copies:
+        cp.start()
+    for cp in copies:
+        cp.wait()
 
 
 def body(row_embed, col_embed, counts, occupancy, row_marg, col_marg, log_total):
@@ -264,43 +287,58 @@
     cfg = (n, d, dp, w, band, rows, tile, q_w,
            1.0 / math.sqrt(w * n * lax.axis_size("col")), 1.0 / math.sqrt(rows * n))
     bf, f32 = jnp.bfloat16, jnp.float32
-    vm, sm, hb = (pl.BlockSpec(memory_space=m) for m in (pltpu.VMEM, pltpu.SMEM, pl.ANY))
+    vm, hb, anywhere = (pl.BlockSpec(memory_space=m) for m in (pltpu.VMEM, pltpu.HBM, pl.ANY))
     dma = lambda *s: pltpu.SemaphoreType.DMA(s) if s else pltpu.SemaphoreType.DMA
+    scratch = [
+        pltpu.VMEM((d, rows), bf),
+        pltpu.VMEM((rows * btiles, LANES), jnp.int32),
+        pltpu.VMEM((dp, rows), bf),
+        pltpu.VMEM((w, dp), f32),
+        pltpu.VMEM((2, n, w, dp), bf),
+        pltpu.VMEM((2, dp, band), bf),
+        pltpu.VMEM((2, nq, band, q_w), bf),
+        pltpu.VMEM((nq, band, q_w), f32),
+        pltpu.VMEM((nq, band, q_w), f32),
+        pltpu.VMEM((band, rows), bf),
+        pltpu.VMEM((n, w, dp), f32),
+        pltpu.VMEM((half, w, dp), f32),
+        pltpu.VMEM((half, w, dp), SEND),
+        pltpu.VMEM((half, w, dp), SEND),
+        pltpu.VMEM((w, d), bf),
+        pltpu.VMEM((occupancy.shape[2], occupancy.shape[0]), jnp.int32),
+        pltpu.VMEM((1, rows), jnp.int32),
+        pltpu.VMEM((1, w), jnp.int32),
+        dma(nq + 5),
+        dma(2, half), dma(2, half), dma(2, half), dma(2, half), dma(), dma(),
+        dma(nq), dma(nq), dma(half), dma(half), dma(half), dma(half),
+    ]
+    limit = min(60 << 20, (6 << 20) + scratch_bytes(scratch[:18]) + 2 * d * rows * 4 + 24 * band * q_w)
     grad_rows, grad_cols = pl.pallas_call(
         functools.partial(kernel, cfg),
         out_shape=(jax.ShapeDtypeStruct((d, rows), f32), jax.ShapeDtypeStruct((w, d), f32)),
-        in_specs=[hb, vm, hb, sm, vm, vm, sm],
+        in_specs=[hb] * 6 + [pl.BlockSpec(memory_space=pltpu.SMEM)],
         out_specs=(vm, vm),
-        scratch_shapes=[
-            pltpu.VMEM((d, rows), bf),
-            pltpu.VMEM((rows * btiles, LANES), jnp.int32),
-            pltpu.VMEM((dp, rows), bf),
-            pltpu.VMEM((w, dp), f32),
-            pltpu.VMEM((2, n, w, dp), bf),
-            pltpu.VMEM((2, dp, band), bf),
-            pltpu.VMEM((2, nq, band, q_w), bf),
-            pltpu.VMEM((nq, band, q_w), f32),
-            pltpu.VMEM((nq, band, q_w), f32),
-            pltpu.VMEM((band, rows), bf),
-            pltpu.VMEM((n, w, dp), f32),
-            pltpu.VMEM((half, w, dp), f32),
-            pltpu.VMEM((half, w, dp), SEND),
-            pltpu.VMEM((half, w, dp), SEND),
-            dma(nq + 1),
-            dma(2, half), dma(2, half), dma(2, half), dma(2, half), dma(), dma(),
-            dma(nq), dma(nq), dma(half), dma(half), dma(half), dma(half),
-        ],
+        scratch_shapes=scratch,
         compiler_params=pltpu.CompilerParams(
-            collective_id=0, has_side_effects=True, vmem_limit_bytes=60 * 1024 * 1024),
+            collective_id=0, has_side_effects=True, vmem_limit_bytes=limit),
     )(
-        row_embed,
-        jnp.transpose(col_embed, (1, 2, 0)).reshape(w, d),
-        counts.reshape(rows * btiles, LANES),
-        jnp.transpose(occupancy, (1, 2, 0)).reshape(occupancy.shape[2], occupancy.shape[0]),
-        row_marg.reshape(1, rows),
-        col_marg,
+        *(pltpu.with_memory_space_constraint(x, pltpu.HBM) for x in (
+            row_embed,
+            jnp.transpose(col_embed, (1, 2, 0)).reshape(w, d),
+            counts.reshape(rows * btiles, LANES),
+            jnp.transpose(occupancy, (1, 2, 0)).reshape(occupancy.shape[2], occupancy.shape[0]),
+            row_marg.reshape(1, rows),
+            col_marg,
+        )),
         log_total,
     )
+    grad_rows, grad_cols = pl.pallas_call(
+        place,
+        out_shape=(jax.ShapeDtypeStruct((d, rows), f32), jax.ShapeDtypeStruct((w, d), f32)),
+        in_specs=[anywhere, anywhere],
+        out_specs=(hb, hb),
+        scratch_shapes=[pltpu.SemaphoreType.DMA((2,))],
+    )(*(pltpu.with_memory_space_constraint(x, pltpu.VMEM) for x in (grad_rows, grad_cols)))
     return grad_rows, jnp.transpose(grad_cols.reshape(1, w, d), (2, 0, 1))
 
 

time: 27.6 us -> 23.7 us (0.86)
  local copies, waits for them, and re-layouts: 3.08 us -> 0 us
  Pallas kernels: 23 us -> 22.2 us
    unnamed x4 -> x0, local copies, waits for them, and re-layouts: 3.08 us -> none
    pallas_call x1, Pallas kernels: 23 us -> 21.2 us  [body(): pl.pallas_call(functools.partial(kernel, cfg), out_shape=(jax.ShapeDtypeS...]
    pallas_call x0 -> x1, Pallas kernels: none -> 1.06 us  [body(): pl.pallas_call(place, out_shape=(jax.ShapeDtypeStruct((d, rows), f32), ja...]
where the time goes in v2:
time: 23.7 us; the launch traced here: 23.5 us
  Pallas kernels  22.2 us (94%)
  between operations  1.29 us (5%)
    pallas_call x1, Pallas kernels, body(): pl.pallas_call(functools.partial(kernel, cfg), out_shape=(jax.ShapeDtypeS...  21.2 us
    pallas_call x1, Pallas kernels, body(): pl.pallas_call(place, out_shape=(jax.ShapeDtypeStruct((d, rows), f32), ja...  1.06 us

profile of v2, /device:TPU:0, one launch (start us, length us, event | category | flops | bytes accessed | tf_op | source)
XLA Modules:
  0.0 23.5 jit_solution(8054018453140022666)
XLA Ops:
  1.3 21.2 %shard_map.86 = (f32[300,1024]{1,0:T(8,128)S(1)}, f32[16,300]{1,0:T(8,128)S(1)}) custom-call(bf16[300,1024]{1,0:T(8,128)(2,1)} %r_hbm.1, bf16[16,300]{1,0:T(8,128)(2,1)} %bitcast.12, s32[2048,128]{1,0:T(8,128)} %bitcast.11, s32[2,8]{1,0:T(2,128)} %bitcast.14, s32[1,1024]{1,0:T(1,128)} %bitcast.13, s32[1,16]{1,0:T(1,128)} %cm_hbm.1, f32[1]{0:T(128)S(6)} %copy.9.lt_ref), custom_call_target="tpu_custom_call" | custom-call | tf_op jit(solution)/shard_map/pallas_call | solution.py:316
  22.5 1.1 %shard_map.87 = (f32[300,1024]{1,0:T(8,128)}, f32[16,300]{1,0:T(8,128)}) custom-call(f32[300,1024]{1,0:T(8,128)S(1)} %get-tuple-element.6.rows_in, f32[16,300]{1,0:T(8,128)S(1)} %get-tuple-element.7.cols_in), custom_call_target="tpu_custom_call" | custom-call | tf_op jit(solution)/shard_map/pallas_call | solution.py:335

commit v3 on v2

--- a/solution.py
+++ b/solution.py
@@ -52,7 +52,7 @@
 def kernel(cfg, r_hbm, c_hbm, cnt_hbm, occ_hbm, rm_hbm, cm_hbm, lt_ref,
            rows_out, cols_out,
            r_v, cnt_v, raug, blk, cg, cd, enc, slope_v, logc_v, res, gcol, s1buf, s2src, s2buf,
-           c_ref, occ_ref, rm_ref, cm_ref, dsem, gz_s, gz_r, gc_s, gc_r, gx_s, gx_r, e_s, e_r, a_s, a_r, b_s, b_r):
+           c_ref, occ_ref, rm_ref, cm_ref, dsem, gz_s, gz_r, gc_s, gc_r, gx_s, gx_r, e_s, e_r, a_s, a_r, b_s, b_r, token):
     n, d, dp, w, band, rows, tile, q_w, scale_r, scale_c = cfg
     half = n // 2
     nq = rows // q_w
@@ -75,7 +75,9 @@
             device_id=dev, device_id_type=pl.DeviceIdType.MESH)
 
     barrier = pltpu.get_barrier_semaphore()
-    for dev in [(p, col) for p in peers] + [at_mate, at_x]:
+    masks = [half >> k for k in range(1, half.bit_length())]
+    near = [(2 * (mine + m - 2 * m * lax.rem(mine // m, 2)) + core, col) for m in masks]
+    for dev in near + [at_mate, at_x]:
         pl.semaphore_signal(barrier, inc=1, device_id=dev, device_id_type=pl.DeviceIdType.MESH)
     small = []
     for k, (src, dst) in enumerate(((cm_hbm, cm_ref), (c_hbm, c_ref), (occ_hbm, occ_ref),
@@ -130,24 +132,47 @@
         for t in range(btiles):
             part(t)
 
+    ecopies = [rcopy(enc.at[0, q], enc.at[1, q], e_s.at[q], e_r.at[q], at_x) for q in range(nq)]
     encode(0)
-    pl.semaphore_wait(barrier, half + 1)
-
+    pl.semaphore_wait(barrier, len(masks) + 2)
+    ecopies[0].start()
     xcp = rcopy(cg.at[0, me], cg.at[1, me], gx_s, gx_r, at_x)
     xcp.start()
     sends = [xcp]
-    for p in peers:
-        cp = rcopy(cg.at[0, me], cg.at[0, me], gz_s.at[0, p // 2], gz_r.at[0, mine], (p, col))
-        cp.start()
-        sends.append(cp)
     cp = rcopy(cg.at[0, me], cg.at[0, me], gc_s.at[0, mine], gc_r.at[0, mine], at_mate)
     cp.start()
     sends.append(cp)
 
-    ecopies = [rcopy(enc.at[0, q], enc.at[1, q], e_s.at[q], e_r.at[q], at_x) for q in range(nq)]
-    for q in range(1, nq):
-        ecopies[q - 1].start()
+    done = 1
+    for k in range(1, len(masks)):
+        pl.semaphore_signal(token.at[k], inc=1, device_id=near[k], device_id_type=pl.DeviceIdType.MESH)
+        if done < nq:
+            encode(done)
+        pl.semaphore_wait(token.at[k], 1)
+        if done < nq:
+            ecopies[done].start()
+            done += 1
+
+    for p in peers:
+        cp = rcopy(cg.at[0, me], cg.at[0, me], gz_s.at[0, p // 2], gz_r.at[0, mine], (p, col))
+        cp.start()
+        sends.append(cp)
+    for q in range(done, nq):
         encode(q)
+        if q > done:
+            ecopies[q - 1].start()
+
+    xcp.wait_recv()
+    for p in peers:
+        cp = rcopy(cg.at[1, me], cg.at[1, me], gz_s.at[1, p // 2], gz_r.at[1, mine], (p, col))
+        cp.start()
+        sends.append(cp)
+    cp = rcopy(cg.at[1, me], cg.at[1, me], gc_s.at[1, mine], gc_r.at[1, mine], at_mate)
+    cp.start()
+    sends.append(cp)
+
+    if done < nq:
+        ecopies[nq - 1].start()
 
     rload.wait()
     raug[pl.ds(0, d), :] = r_v[...]
@@ -160,16 +185,6 @@
     for at, val in ((d + 3, hi), (d + 4, mid), (d + 5, lo)):
         tail = jnp.where(si == at, val, tail)
     raug[pl.ds(first, dp - first), :] = tail.astype(jnp.bfloat16)
-    ecopies[nq - 1].start()
-
-    xcp.wait_recv()
-    for p in peers:
-        cp = rcopy(cg.at[1, me], cg.at[1, me], gz_s.at[1, p // 2], gz_r.at[1, mine], (p, col))
-        cp.start()
-        sends.append(cp)
-    cp = rcopy(cg.at[1, me], cg.at[1, me], gc_s.at[1, mine], gc_r.at[1, mine], at_mate)
-    cp.start()
-    sends.append(cp)
 
     def forward(which):
         for p in froms:
@@ -209,7 +224,8 @@
         gcol[pl.ds(s * per, per)] = nt(res[pl.ds(s * sub, sub), :], raug[...]).reshape(per, w, dp)
 
     repeat(nsub, col_terms)
-    for k in range(half):
+    for p in peers + [me]:
+        k = p // 2
         cp = rcopy(gcol.at[2 * k + 1 - core], s1buf.at[k], a_s.at[k], a_r.at[k], at_mate)
         cp.start()
         sends.append(cp)
@@ -225,18 +241,21 @@
     transposed(0)
     rows_out[...] = nn(cd[0], res[...])[:d, :]
 
+    held = None
+    for p in peers + [me]:
+        rcopy(gcol.at[p], s1buf.at[p // 2], a_s.at[p // 2], a_r.at[p // 2], at_mate).wait_recv()
+        if p is me:
+            total = gcol[me] + s1buf[mine]
+        else:
+            s2src[p // 2] = (gcol[p] + s1buf[p // 2]).astype(s2src.dtype)
+        if held is not None:
+            held.start()
+            sends.append(held)
+        held = None if p is me else rcopy(
+            s2src.at[p // 2], s2buf.at[mine], b_s.at[p // 2], b_r.at[mine], (p, col))
+
     forward(1)
-    for k in range(half):
-        rcopy(gcol.at[k], s1buf.at[k], a_s.at[k], a_r.at[k], at_mate).wait_recv()
-    for p in peers:
-        s2src[p // 2] = (gcol[p] + s1buf[p // 2]).astype(s2src.dtype)
-    total = gcol[me] + s1buf[mine]
     mate_blocks(1)
-    for p in peers:
-        cp = rcopy(s2src.at[p // 2], s2buf.at[mine], b_s.at[p // 2], b_r.at[mine], (p, col))
-        cp.start()
-        sends.append(cp)
-
     transposed(1)
     for q in range(nq):
         qs = pl.ds(q * q_w, q_w)
@@ -311,6 +330,7 @@
         dma(nq + 5),
         dma(2, half), dma(2, half), dma(2, half), dma(2, half), dma(), dma(),
         dma(nq), dma(nq), dma(half), dma(half), dma(half), dma(half),
+        pltpu.SemaphoreType.REGULAR((half.bit_length() - 1,)),
     ]
     limit = min(60 << 20, (6 << 20) + scratch_bytes(scratch[:18]) + 2 * d * rows * 4 + 24 * band * q_w)
     grad_rows, grad_cols = pl.pallas_call(

time: 23.7 us -> 23.2 us (0.979)
  Pallas kernels: 22.2 us -> 21.8 us
    pallas_call x1, Pallas kernels: 21.2 us -> 20.7 us  [body(): pl.pallas_call(functools.partial(kernel, cfg), out_shape=(jax.ShapeDtypeS...]
where the time goes in v3:
time: 23.2 us; the launch traced here: 23.1 us
  Pallas kernels  21.8 us (94%)
  between operations  1.29 us (6%)
    pallas_call x1, Pallas kernels, body(): pl.pallas_call(functools.partial(kernel, cfg), out_shape=(jax.ShapeDtypeS...  20.7 us
    pallas_call x1, Pallas kernels, body(): pl.pallas_call(place, out_shape=(jax.ShapeDtypeStruct((d, rows), f32), ja...  1.06 us

profile of v3, /device:TPU:0, one launch (start us, length us, event | category | flops | bytes accessed | tf_op | source)
XLA Modules:
  0.0 23.1 jit_solution(12481788627422227711)
XLA Ops:
  1.3 20.7 %shard_map.86 = (f32[300,1024]{1,0:T(8,128)S(1)}, f32[16,300]{1,0:T(8,128)S(1)}) custom-call(bf16[300,1024]{1,0:T(8,128)(2,1)} %r_hbm.1, bf16[16,300]{1,0:T(8,128)(2,1)} %bitcast.12, s32[2048,128]{1,0:T(8,128)} %bitcast.11, s32[2,8]{1,0:T(2,128)} %bitcast.14, s32[1,1024]{1,0:T(1,128)} %bitcast.13, s32[1,16]{1,0:T(1,128)} %cm_hbm.1, f32[1]{0:T(128)S(6)} %copy.9.lt_ref), custom_call_target="tpu_custom_call" | custom-call | tf_op jit(solution)/shard_map/pallas_call | solution.py:336
  22.0 1.1 %shard_map.87 = (f32[300,1024]{1,0:T(8,128)}, f32[16,300]{1,0:T(8,128)}) custom-call(f32[300,1024]{1,0:T(8,128)S(1)} %get-tuple-element.6.rows_in, f32[16,300]{1,0:T(8,128)S(1)} %get-tuple-element.7.cols_in), custom_call_target="tpu_custom_call" | custom-call | tf_op jit(solution)/shard_map/pallas_call | solution.py:355
